TPU v7x, 256 devices: a whole 4x4x8 slice. The times are simulated.
256 devices in a mesh: tm: 8 (over y, x_lo), space: 32 (over z, x_hi, core).
Axes of the slice: x: 4 (x_hi: 2, x_lo: 2; x = x_hi * 2 + x_lo), y: 4, z: 8, core: 2. Of those that a mesh axis runs over, the one named last changes fastest.
Arguments:
- density: float32 [128, 512, 1024], P('tm', 'space'), may hold values from 0.2 to 2
- flux_x: float32 [128, 512, 1024], P('tm', 'space'), may hold values from -3 to 3
- flux_y: float32 [128, 512, 1024], P('tm', 'space'), may hold values from -3 to 3
- source: float32 [128, 512, 1024], P('tm', 'space'), may hold values from -3 to 3
- potential: float32 [128, 512, 1024], P('tm', 'space'), may hold values from -6 to 6
- start_density: float32 [512, 1024], P('space'), may hold values from 0.2 to 2
- end_density: float32 [512, 1024], P('space'), may hold values from 0.2 to 2
Outputs:
- final_density: float32 [128, 512, 1024], P('tm', 'space')
- final_flux_x: float32 [128, 512, 1024], P('tm', 'space')
- final_flux_y: float32 [128, 512, 1024], P('tm', 'space')
- final_source: float32 [128, 512, 1024], P('tm', 'space')
- final_potential: float32 [128, 512, 1024], P('tm', 'space')
All inputs are finite; a program needn't handle non-finite values.
Results may differ from a plain program's by a relative error of at most 0.00002.
Values sent between devices are 32-bit elements; how exact they have to be, the bound alone decides.
A program may use at most 64 MiB of HBM per device.

v0:
```python
import functools

import jax
import jax.numpy as jnp
from jax import lax
from jax.experimental import pallas as pl
from jax.experimental.pallas import tpu as pltpu
from jax.sharding import PartitionSpec as P

NEWTON = 8
ITERS = 6

tau_step = 0.04
end_weight = 10.0

T = 16
R = 16
PAIRS = T // 2
BLOCK = 8
TILE = (8, 128)
MESH = pl.DeviceIdType.MESH


def previous_column(x):
    moved = pltpu.roll(x, 1, 2)
    lane = lax.broadcasted_iota(jnp.int32, x.shape, 2)
    return jnp.where(lane == 0, pltpu.roll(moved, 1, 1), moved)


def next_column(x):
    moved = pltpu.roll(x, 127, 2)
    lane = lax.broadcasted_iota(jnp.int32, x.shape, 2)
    return jnp.where(lane == 127, pltpu.roll(moved, 7, 1), moved)


def newton(top, energy):
    twice = tau_step * energy
    thrice = (1.5 * tau_step) * energy
    q = jnp.maximum(top, tau_step)
    for repeat in range(NEWTON):
        square = q * q
        step = (top * square + thrice) / (square * q + twice)
        q = jnp.maximum(step * q, tau_step)
    root = q - tau_step
    return root, root / q


def kernel(
    sizes,
    rho_in, fx_in, fy_in, src_in, pot_in, start_in, end_in,
    rho_out, fx_out, fy_out, src_out, pot_out,
    raw, edge, pot, psi, bar_rho, bar_fx, rho, fx, fy, src, start, end,
    plane_out, fx_rows_out, pot_rows_out,
    rho_halo, pot_halo, fx_rows, pot_rows, fx_corner, rho_corner,
    in_sem, edge_sem, out_sem,
    plane_send, fx_send, pot_send,
    plane_recv, fx_recv, pot_recv,
):
    n_time, n_space = sizes
    me_time, me_space = lax.axis_index("tm"), lax.axis_index("space")
    time_next = lax.rem(me_time + 1, n_time)
    time_prev = lax.rem(me_time + n_time - 1, n_time)
    space_next = lax.rem(me_space + 1, n_space)
    space_prev = lax.rem(me_space + n_space - 1, n_space)
    first = me_time == 0
    last = me_time == n_time - 1

    fields_in = (rho_in, fx_in, fy_in, src_in, pot_in)
    fields_out = (rho_out, fx_out, fy_out, src_out, pot_out)
    plane_rows = R * 8

    def plane_in(n, t):
        rows = pl.ds(t * plane_rows, plane_rows)
        return pltpu.make_async_copy(fields_in[n].at[rows], raw.at[n, rows], in_sem.at[n, t])

    def plane_result(n, t):
        rows = pl.ds(t * plane_rows, plane_rows)
        return pltpu.make_async_copy(raw.at[n, rows], fields_out[n].at[rows], out_sem.at[n, t])

    def edge_in(n):
        return pltpu.make_async_copy((start_in, end_in)[n], edge.at[n], edge_sem.at[n])

    for n in range(2):
        edge_in(n).start()
    for u in range(PAIRS):
        for t in (u, T - 1 - u):
            for n in range(5):
                plane_in(n, t).start()

    barrier = pltpu.get_barrier_semaphore()
    partners = (
        (time_next, me_space), (time_prev, me_space),
        (me_time, space_next), (me_time, space_prev),
        (time_prev, space_next), (time_next, space_prev),
    )
    for partner in partners:
        pl.semaphore_signal(barrier, inc=1, device_id=partner, device_id_type=MESH)
    pl.semaphore_wait(barrier, len(partners))

    def send(source, target, send_sem, recv_sem, device):
        return pltpu.make_async_remote_copy(
            src_ref=source, dst_ref=target, send_sem=send_sem, recv_sem=recv_sem,
            device_id=device, device_id_type=MESH,
        )

    def send_rho(slot):
        return send(bar_rho.at[T - 1], rho_halo.at[slot], plane_send.at[0], plane_recv.at[slot, 0], (time_next, me_space))

    def send_pot(slot):
        return send(plane_out, pot_halo.at[slot], plane_send.at[1], plane_recv.at[slot, 1], (time_prev, me_space))

    def send_fx_corner(slot):
        return send(fx_rows_out.at[0], fx_corner.at[slot], plane_send.at[2], plane_recv.at[slot, 2], (time_prev, space_next))

    def send_rho_corner(slot):
        return send(bar_rho.at[T - 1, 0], rho_corner.at[slot], plane_send.at[3], plane_recv.at[slot, 3], (time_next, space_prev))

    def send_fx_rows(slot, u):
        rows = pl.ds(2 * u, 2)
        return send(fx_rows_out.at[rows], fx_rows.at[slot, rows], fx_send.at[u], fx_recv.at[slot, u], (me_time, space_next))

    def send_pot_rows(slot, u):
        rows = pl.ds(2 * u, 2)
        return send(pot_rows_out.at[rows], pot_rows.at[slot, rows], pot_send.at[u], pot_recv.at[slot, u], (me_time, space_prev))

    def send_pot_first(slot):
        rows = pl.ds(0, 1)
        return send(pot_rows_out.at[rows], pot_rows.at[slot, rows], pot_send.at[0], pot_recv.at[slot, 0], (me_time, space_prev))

    def send_pot_last(slot):
        rows = pl.ds(2 * PAIRS + 1, 1)
        return send(
            pot_rows_out.at[rows], pot_rows.at[slot, rows], pot_send.at[PAIRS], pot_recv.at[slot, PAIRS], (me_time, space_prev)
        )

    def emit_first(slot):
        plane_out[0] = pot[0, 0]
        plane_out[1:R] = pot[0, 1:R] - bar_fx[0, 0 : R - 1]
        fx_rows_out[0] = bar_fx[0, R - 1]
        fx_rows_out[1] = bar_fx[T - 1, R - 1]
        pot_rows_out[0] = pot[0, 0] - jnp.where(first, start[0], jnp.zeros(TILE, jnp.float32))
        send_pot(slot).start()
        send_rho(slot).start()
        send_fx_corner(slot).start()
        send_rho_corner(slot).start()
        send_fx_rows(slot, 0).start()
        send_pot_first(slot).start()

    def emit(slot, u):
        fx_rows_out[2 * u] = bar_fx[u, R - 1]
        fx_rows_out[2 * u + 1] = bar_fx[T - 1 - u, R - 1]
        pot_rows_out[2 * u] = pot[u, 0] - bar_rho[u - 1, 0]
        pot_rows_out[2 * u + 1] = pot[T - u, 0] - bar_rho[T - 1 - u, 0]
        send_fx_rows(slot, u).start()
        send_pot_rows(slot, u).start()

    def emit_last(slot):
        pot_rows_out[2 * PAIRS + 1] = pot[PAIRS, 0] - bar_rho[PAIRS - 1, 0]
        send_pot_last(slot).start()

    def divergence(b_rho, b_fx, b_fy, b_src):
        return b_rho + b_fx + (b_fy - previous_column(b_fy)) - b_src

    for n, ref in enumerate((start, end)):
        edge_in(n).wait()
        for i in range(R):
            ref[i] = edge[n, pl.ds((i // 8) * 64 + i % 8, 8, stride=8), :]

    def load_plane(t):
        for n in range(5):
            plane_in(n, t).wait()

        for i in range(R):
            rows = pl.ds(t * plane_rows + (i // 8) * 64 + i % 8, 8, stride=8)
            d, x, y, s, p = (raw[n, rows, :] for n in range(5))
            rho[t, i] = d
            fx[t, i] = x
            fy[t, i] = y
            src[t, i] = s
            bar_rho[t, i] = d
            bar_fx[t, i] = x
            pot[t, i] = p + divergence(d[None], x[None], y[None], s[None])[0]

    load_plane(0)
    load_plane(T - 1)
    emit_first(0)

    def load_pair(u, carry):
        load_plane(u)
        load_plane(T - 1 - u)
        emit(0, u)
        return carry

    lax.fori_loop(1, PAIRS, load_pair, 0)
    emit_last(0)

    def store_potential(t, new):
        pot[t] = new
        psi[t, 0:R] = tau_step * new

    def potential(t, slot, halo):
        below = bar_rho[t - 1]
        pot_0 = pot[t, 0] - below[0] - fx_rows[slot, halo]
        pot_n = pot[t, 1:R] - below[1:R] - bar_fx[t, 0 : R - 1]
        pot[t, 0] = pot_0
        pot[t, 1:R] = pot_n
        psi[t, 0] = tau_step * pot_0
        psi[t, 1:R] = tau_step * pot_n

    def update(t, final, end_scale=None, end_pull=None):
        for i0 in range(0, R, BLOCK):
            rows = pl.ds(i0, BLOCK)
            here = psi[t, rows]
            old = rho[t, rows], fx[t, rows], fy[t, rows], src[t, rows]
            target = old[0] - (here - psi[t + 1, rows])
            moved_fx = old[1] - (here - psi[t, pl.ds(i0 + 1, BLOCK)])
            moved_fy = old[2] - (here - next_column(here))
            moved_src = old[3] + here
            energy = moved_fx * moved_fx + moved_fy * moved_fy + moved_src * moved_src
            if end_scale is not None:
                target = (target + end_pull * end[rows]) * end_scale
                energy = energy * end_scale
            root, factor = newton(target + tau_step, energy)
            new = root, factor * moved_fx, factor * moved_fy, factor * moved_src
            if final:
                for n, value in enumerate(new + (pot[t, rows],)):
                    for i in range(BLOCK):
                        row = i0 + i
                        raw[n, pl.ds(t * plane_rows + (row // 8) * 64 + row % 8, 8, stride=8), :] = value[i]
            else:
                bars = tuple(fresh + (fresh - older) for fresh, older in zip(new, old))
                rho[t, rows], fx[t, rows], fy[t, rows], src[t, rows] = new
                pot[t, rows] = pot[t, rows] + divergence(*bars)
                bar_rho[t, rows] = bars[0]
                bar_fx[t, rows] = bars[1]

    def next_row_halo(t, slot, row, corner=None):
        value = pot_rows[slot, row] - bar_fx[t, R - 1]
        if corner is not None:
            value = value - corner
        psi[t, R] = tau_step * value

    def first_pair(now, later, final):
        send_fx_rows(now, 0).wait_recv()
        send_fx_rows(now, 1).wait_recv()
        send_rho(now).wait_recv()
        send_pot(now).wait_recv()
        send_fx_corner(now).wait_recv()
        before = jnp.where(first, start[...], rho_halo[now])
        pot_0 = pot[0, 0] - before[0] - fx_rows[now, 0]
        pot_n = pot[0, 1:R] - before[1:R] - bar_fx[0, 0 : R - 1]
        pot[0, 0] = pot_0
        pot[0, 1:R] = pot_n
        psi[0, 0] = tau_step * pot_0
        psi[0, 1:R] = tau_step * pot_n
        above = pot_halo[now] - bar_rho[T - 1]
        psi[T, 0:R] = jnp.where(last, jnp.zeros_like(above), tau_step * above)
        corner = psi[T, 0] - tau_step * fx_corner[now]
        psi[T, 0] = jnp.where(last, jnp.zeros_like(corner), corner)
        potential(1, now, 2)
        potential(T - 1, now, 1)
        send_pot_first(now).wait_recv()
        send_pot_rows(now, 1).wait_recv()
        send_rho_corner(now).wait_recv()
        next_row_halo(0, now, 0, jnp.where(first, jnp.zeros(TILE, jnp.float32), rho_corner[now]))
        next_row_halo(T - 1, now, 3)
        send_rho(now).wait_send()
        send_pot(now).wait_send()
        send_fx_corner(now).wait_send()
        send_rho_corner(now).wait_send()
        send_fx_rows(now, 0).wait_send()
        send_pot_first(now).wait_send()
        update(0, final)
        scale = jnp.where(last, 1.0 / (1.0 + tau_step * end_weight), 1.0).astype(jnp.float32)
        pull = jnp.where(last, tau_step * end_weight, 0.0).astype(jnp.float32)
        update(T - 1, final, scale, pull)
        if final:
            write_pair(0)
        else:
            emit_first(later)

    def write_pair(u):
        for t in (u, T - 1 - u):
            for n in range(5):
                plane_result(n, t).start()

    def middle_pair(u, now, later, final):
        @pl.when(u < PAIRS - 1)
        def _():
            send_fx_rows(now, u + 1).wait_recv()
            potential(u + 1, now, 2 * u + 2)
            send_pot_rows(now, u + 1).wait_recv()

        @pl.when(u == PAIRS - 1)
        def _():
            send_pot_last(now).wait_recv()

        potential(T - 1 - u, now, 2 * u + 1)
        next_row_halo(u, now, 2 * u)
        next_row_halo(T - 1 - u, now, 2 * u + 3)
        send_fx_rows(now, u).wait_send()
        send_pot_rows(now, u).wait_send()
        update(u, final)
        update(T - 1 - u, final)
        if final:
            write_pair(u)
        else:
            emit(later, u)

    def iteration(now, later, final):
        first_pair(now, later, final)

        def pair(u, carry):
            middle_pair(u, now, later, final)
            return carry

        lax.fori_loop(1, PAIRS, pair, 0)
        send_pot_last(now).wait_send()
        if not final:
            emit_last(later)

    def step(k, carry):
        iteration(lax.rem(k - 1, 2), lax.rem(k, 2), False)
        return carry

    lax.fori_loop(1, ITERS, step, 0)
    iteration((ITERS - 1) % 2, None, True)

    for t in range(T):
        for n in range(5):
            plane_result(n, t).wait()


def to_rows(x):
    planes = x.shape[0]
    return x.reshape(planes, R // 8, 8, 8, 128).transpose(0, 1, 3, 2, 4).reshape(planes * R * 8, 128)


def from_rows(x):
    return x.reshape(T, R // 8, 8, 8, 128).transpose(0, 1, 3, 2, 4).reshape(T, R, 1024)


def solution(mesh):
    sizes = mesh.shape["tm"], mesh.shape["space"]
    f32 = jnp.float32
    vmem = pltpu.VMEM
    dma = pltpu.SemaphoreType.DMA

    def body(density, flux_x, flux_y, source, potential, start_density, end_density):
        anywhere = pl.BlockSpec(memory_space=pl.ANY)
        rows = T * R * 8
        results = pl.pallas_call(
            functools.partial(kernel, sizes),
            out_shape=[jax.ShapeDtypeStruct((rows, 128), f32)] * 5,
            in_specs=[anywhere] * 7,
            out_specs=[anywhere] * 5,
            scratch_shapes=[
                vmem((5, rows, 128), f32),
                vmem((2, R * 8, 128), f32),
                vmem((T, R) + TILE, f32),
                vmem((T + 1, R + 1) + TILE, f32),
                vmem((T, R) + TILE, f32),
                vmem((T, R) + TILE, f32),
                vmem((T, R) + TILE, f32),
                vmem((T, R) + TILE, f32),
                vmem((T, R) + TILE, f32),
                vmem((T, R) + TILE, f32),
                vmem((R,) + TILE, f32),
                vmem((R,) + TILE, f32),
                vmem((R,) + TILE, f32),
                vmem((2 * PAIRS,) + TILE, f32),
                vmem((2 * PAIRS + 2,) + TILE, f32),
                vmem((2, R) + TILE, f32),
                vmem((2, R) + TILE, f32),
                vmem((2, 2 * PAIRS) + TILE, f32),
                vmem((2, 2 * PAIRS + 2) + TILE, f32),
                vmem((2,) + TILE, f32),
                vmem((2,) + TILE, f32),
                dma((5, T)),
                dma((2,)),
                dma((5, T)),
                dma((4,)),
                dma((PAIRS,)),
                dma((PAIRS + 1,)),
                dma((2, 4)),
                dma((2, PAIRS)),
                dma((2, PAIRS + 1)),
            ],
            compiler_params=pltpu.CompilerParams(collective_id=0, has_side_effects=True),
        )(
            *(to_rows(x) for x in (density, flux_x, flux_y, source, potential)),
            to_rows(start_density[None]),
            to_rows(end_density[None]),
        )
        return tuple(from_rows(x) for x in results)

    volume, plane = P("tm", "space", None), P("space", None)
    return jax.shard_map(
        body, mesh=mesh, in_specs=(volume,) * 5 + (plane,) * 2, out_specs=(volume,) * 5, check_vma=False
    )
```

profile of v0, /device:TPU:1, one launch (start us, length us, event | category | flops | bytes accessed | tf_op | source)
XLA Modules:
  0.0 65.2 jit_solution(6644213724617338591)
XLA Ops:
  0.6 56.4 %shard_map.110 = (f32[2048,128]{1,0:T(8,128)}, f32[2048,128]{1,0:T(8,128)}, f32[2048,128]{1,0:T(8,128)}, f32[2048,128]{1,0:T(8,128)}, f32[2048,128]{1,0:T(8,128)}) custom-call(f32[2048,128]{1,0:T(8,128)} %bitcast.65, f32[2048,128]{1,0:T(8,128)} %bitcast.66, f32[2048,128]{1,0:T(8,128)} %bitcast.67, f32[2048,128]{1,0:T(8,128)} %bitcast.68, ...), custom_call_target="tpu_custom_call" | custom-call | tf_op jit(solution)/shard_map/pallas_call | solution.py:352
  57.0 0.0 copy-start.3
  57.0 2.4 %copy.17 = f32[16,16,1024]{2,1,0:T(8,128)} copy(f32[16,16,1024]{2,1,0:T(8,128)} %bitcast.64) | data formatting | bytes 2097152
  59.4 0.0 copy-done.3
  59.4 0.0 copy-start.2
  59.4 1.0 %copy.18 = f32[16,16,1024]{2,1,0:T(8,128)} copy(f32[16,16,1024]{2,1,0:T(8,128)S(1)} %bitcast.63) | data formatting | bytes 2097152
  60.4 0.6 copy-done.2
  61.0 0.0 copy-start.1
  61.0 1.0 %copy.19 = f32[16,16,1024]{2,1,0:T(8,128)} copy(f32[16,16,1024]{2,1,0:T(8,128)S(1)} %bitcast.62) | data formatting | bytes 2097152
  62.0 0.6 copy-done.1
  62.6 0.0 copy-start
  62.6 1.0 %copy.20 = f32[16,16,1024]{2,1,0:T(8,128)} copy(f32[16,16,1024]{2,1,0:T(8,128)S(1)} %bitcast.61) | data formatting | bytes 2097152
  63.6 0.6 copy-done
  64.2 1.0 %copy.21 = f32[16,16,1024]{2,1,0:T(8,128)} copy(f32[16,16,1024]{2,1,0:T(8,128)S(1)} %bitcast.60) | data formatting | bytes 2097152
Async XLA Ops:
  57.0 2.4 %copy-start.3 = (f32[2048,128]{1,0:T(8,128)S(1)}, f32[2048,128]{1,0:T(8,128)}, u32[]{:S(2)}) copy-start(f32[2048,128]{1,0:T(8,128)} %get-tuple-element.11) | copy-start | bytes 3145732
  59.4 1.6 %copy-start.2 = (f32[2048,128]{1,0:T(8,128)S(1)}, f32[2048,128]{1,0:T(8,128)}, u32[]{:S(2)}) copy-start(f32[2048,128]{1,0:T(8,128)} %get-tuple-element.12) | copy-start | bytes 3145732
  61.0 1.6 %copy-start.1 = (f32[2048,128]{1,0:T(8,128)S(1)}, f32[2048,128]{1,0:T(8,128)}, u32[]{:S(2)}) copy-start(f32[2048,128]{1,0:T(8,128)} %get-tuple-element.13) | copy-start | bytes 3145732
  62.6 1.6 %copy-start = (f32[2048,128]{1,0:T(8,128)S(1)}, f32[2048,128]{1,0:T(8,128)}, u32[]{:S(2)}) copy-start(f32[2048,128]{1,0:T(8,128)} %get-tuple-element.14) | copy-start | bytes 3145732
where the time goes:
time: 65.5 us; the launch traced here: 65.2 us
  Pallas kernels  56.4 us (86%)
  local copies, waits for them, and re-layouts  8.18 us (12%)
  between operations  0.66 us (1%)
    pallas_call x1, Pallas kernels, body(): pl.pallas_call(functools.partial(kernel, sizes), out_shape=[jax.ShapeDtyp...  56.4 us
    unnamed x13, local copies, waits for them, and re-layouts  8.18 us

commit v1 on v0

v1 whole, which is shorter than its diff:
```python
import collections
import functools

import jax
import jax.numpy as jnp
from jax import lax
from jax.experimental import pallas as pl
from jax.experimental.pallas import tpu as pltpu
from jax.sharding import PartitionSpec as P

NEWTON = 8
ITERS = 6

tau_step = 0.04
end_weight = 10.0

T = 16
R = 16
PAIRS = T // 2
TILE = (8, 128)
MESH = pl.DeviceIdType.MESH


Half = collections.namedtuple("Half", ("rho", "fx", "fy", "src", "part", "pot", "psi"))


def previous_column(x):
    moved = pltpu.roll(x, 1, 2)
    lane = lax.broadcasted_iota(jnp.int32, x.shape, 2)
    return jnp.where(lane == 0, pltpu.roll(moved, 1, 1), moved)


def next_column(x):
    moved = pltpu.roll(x, 127, 2)
    lane = lax.broadcasted_iota(jnp.int32, x.shape, 2)
    return jnp.where(lane == 127, pltpu.roll(moved, 7, 1), moved)


unit = 1.0 / tau_step


def newton(top, energy):
    half = 0.5 * energy
    thrice = energy + half
    q = jnp.maximum(top, 1.0)
    top = jnp.maximum(top, 1.0 - half)
    for repeat in range(NEWTON):
        square = q * q
        q = (top * square + thrice) / (square * q + energy) * q
    q = jnp.maximum(q, 1.0)
    return q, (q - 1.0) / q


def kernel(
    sizes,
    rho_in, fx_in, fy_in, src_in, pot_in, start_in, end_in,
    rho_out, fx_out, fy_out, src_out, pot_out,
    raw, edge, lower_refs, upper_refs, start, end,
    plane_out, fx_rows_out, pot_rows_out,
    rho_halo, pot_halo, fx_rows, pot_rows, fx_corner, rho_corner,
    in_sem, edge_sem,
    plane_send, fx_send, pot_send,
    plane_recv, fx_recv, pot_recv,
):
    lower, upper = Half(*lower_refs), Half(*upper_refs)
    n_time, n_space = sizes
    me_time, me_space = lax.axis_index("tm"), lax.axis_index("space")
    time_next = lax.rem(me_time + 1, n_time)
    time_prev = lax.rem(me_time + n_time - 1, n_time)
    space_next = lax.rem(me_space + 1, n_space)
    space_prev = lax.rem(me_space + n_space - 1, n_space)
    first = me_time == 0
    last = me_time == n_time - 1

    fields_in = (rho_in, fx_in, fy_in, src_in, pot_in)
    fields_out = (rho_out, fx_out, fy_out, src_out, pot_out)
    plane_rows = R * 8

    def plane_in(n, t):
        rows = pl.ds(t * plane_rows, plane_rows)
        return pltpu.make_async_copy(fields_in[n].at[rows], raw.at[n, rows], in_sem.at[n, t])

    def edge_in(n):
        return pltpu.make_async_copy((start_in, end_in)[n], edge.at[n], edge_sem.at[n])

    barrier = pltpu.get_barrier_semaphore()
    partners = (
        (time_next, me_space), (time_prev, me_space),
        (me_time, space_next), (me_time, space_prev),
        (time_prev, space_next), (time_next, space_prev),
    )
    for partner in partners:
        pl.semaphore_signal(barrier, inc=1, device_id=partner, device_id_type=MESH)

    for u in range(PAIRS):
        for t in (u, T - 1 - u):
            for n in range(5):
                plane_in(n, t).start()
        if u == 0:
            for n in range(2):
                edge_in(n).start()

    def send(source, target, send_sem, recv_sem, device):
        return pltpu.make_async_remote_copy(
            src_ref=source, dst_ref=target, send_sem=send_sem, recv_sem=recv_sem,
            device_id=device, device_id_type=MESH,
        )

    def send_rho(slot):
        return send(upper.rho.at[0], rho_halo.at[slot], plane_send.at[0], plane_recv.at[slot, 0], (time_next, me_space))

    def send_pot(slot):
        return send(plane_out, pot_halo.at[slot], plane_send.at[1], plane_recv.at[slot, 1], (time_prev, me_space))

    def send_fx_corner(slot):
        return send(fx_rows_out.at[0], fx_corner.at[slot], plane_send.at[2], plane_recv.at[slot, 2], (time_prev, space_next))

    def send_rho_corner(slot):
        return send(upper.rho.at[0, 0], rho_corner.at[slot], plane_send.at[3], plane_recv.at[slot, 3], (time_next, space_prev))

    def send_fx_rows(slot, u):
        rows = pl.ds(2 * u, 2)
        return send(fx_rows_out.at[rows], fx_rows.at[slot, rows], fx_send.at[u], fx_recv.at[slot, u], (me_time, space_next))

    def send_pot_rows(slot, u):
        rows = pl.ds(2 * u, 2)
        return send(pot_rows_out.at[rows], pot_rows.at[slot, rows], pot_send.at[u], pot_recv.at[slot, u], (me_time, space_prev))

    def send_pot_first(slot):
        rows = pl.ds(0, 1)
        return send(pot_rows_out.at[rows], pot_rows.at[slot, rows], pot_send.at[0], pot_recv.at[slot, 0], (me_time, space_prev))

    def send_pot_last(slot):
        rows = pl.ds(2 * PAIRS + 1, 1)
        return send(
            pot_rows_out.at[rows], pot_rows.at[slot, rows], pot_send.at[PAIRS], pot_recv.at[slot, PAIRS], (me_time, space_prev)
        )

    def emit_first(slot, gain):
        part, pot, fx = lower.part, lower.pot, lower.fx
        plane_out[0] = pot[0, 0] + gain * part[0, 0]
        plane_out[1:R] = pot[0, 1:R] + gain * (part[0, 1:R] - fx[0, 0 : R - 1])
        fx_rows_out[0] = fx[0, R - 1]
        fx_rows_out[1] = upper.fx[0, R - 1]
        held = jnp.where(first, start[0], jnp.zeros(TILE, jnp.float32))
        pot_rows_out[0] = pot[0, 0] + gain * (part[0, 0] - held)
        send_fx_corner(slot).start()
        send_rho_corner(slot).start()
        send_fx_rows(slot, 0).start()
        send_pot_first(slot).start()
        send_pot(slot).start()
        send_rho(slot).start()

    def emit(slot, u, gain):
        fx_rows_out[2 * u] = lower.fx[u, R - 1]
        fx_rows_out[2 * u + 1] = upper.fx[u, R - 1]
        pot_rows_out[2 * u] = lower.pot[u, 0] + gain * (lower.part[u, 0] - lower.rho[u - 1, 0])
        pot_rows_out[2 * u + 1] = upper.pot[u - 1, 0] + gain * (upper.part[u - 1, 0] - upper.rho[u, 0])
        send_fx_rows(slot, u).start()
        send_pot_rows(slot, u).start()

    def emit_last(slot, gain):
        u = PAIRS - 1
        pot_rows_out[2 * PAIRS + 1] = upper.pot[u, 0] + gain * (upper.part[u, 0] - lower.rho[u, 0])
        send_pot_last(slot).start()

    for n, ref in enumerate((start, end)):
        edge_in(n).wait()
        for i in range(R):
            value = edge[n, pl.ds((i // 8) * 64 + i % 8, 8, stride=8), :]
            ref[i] = value * unit + (1.0 if n == 0 else 0.0)

    def load_plane(t, half, u):
        for n in range(5):
            plane_in(n, t).wait()
        for i in range(R):
            rows = pl.ds(t * plane_rows + (i // 8) * 64 + i % 8, 8, stride=8)
            d, x, y, s, p = (unit * raw[n, rows, :] for n in range(5))
            d = d + 1.0
            half.rho[u, i] = d
            half.fx[u, i] = x
            half.fy[u, i] = y
            half.src[u, i] = s
            half.pot[u, i] = p
            half.part[u, i] = d + x + (y - previous_column(y[None])[0]) - s

    load_plane(0, lower, 0)
    load_plane(T - 1, upper, 0)
    pl.semaphore_wait(barrier, len(partners))
    emit_first(0, 1.0)

    def load_pair(u, carry):
        load_plane(u, lower, u)
        load_plane(T - 1 - u, upper, u)
        emit(0, u, 1.0)
        return carry

    lax.fori_loop(1, PAIRS, load_pair, 0)
    emit_last(0, 1.0)

    def potential(half, u, keep, below, row):
        beside = jnp.concatenate([row[None], half.fx[u, 0 : R - 1]], 0)
        gap = half.part[u] - (below + beside)
        base = half.pot[u] + keep * gap
        half.pot[u] = base
        new = tau_step * (base + gap)
        half.psi[u] = new
        return new

    def update(half, u, t, final, here, above, row, end_scale=None, end_pull=None):
        top = half.rho[u] - (here - above)
        moved_fx = half.fx[u] - (here - jnp.concatenate([here[1:R], row[None]], 0))
        moved_fy = half.fy[u] - (here - next_column(here))
        moved_src = half.src[u] + here
        energy = moved_fx * moved_fx + moved_fy * moved_fy + moved_src * moved_src
        if end_scale is not None:
            top = (top - 1.0 + end_pull * end[...]) * end_scale + 1.0
            energy = energy * end_scale
        q, factor = newton(top, energy)
        new_fx, new_fy, new_src = factor * moved_fx, factor * moved_fy, factor * moved_src
        if final:
            results = tau_step * (q - 1.0), tau_step * new_fx, tau_step * new_fy, tau_step * new_src, here
            for ref, value in zip((rho_out, fx_out, fy_out, src_out, pot_out), results):
                for i in range(R):
                    ref[pl.ds(t * plane_rows + (i // 8) * 64 + i % 8, 8, stride=8), :] = value[i]
        else:
            half.rho[u], half.fx[u], half.fy[u], half.src[u] = q, new_fx, new_fy, new_src
            half.part[u] = q + new_fx + (new_fy - previous_column(new_fy)) - new_src

    def halo_row(half, u, slot, row, gain, corner=None):
        held = half.fx[u, R - 1]
        if corner is not None:
            held = held + corner
        return tau_step * (pot_rows[slot, row] - gain * held)

    def first_pair(now, later, gain, final):
        keep = gain - 1.0
        send_fx_rows(now, 0).wait_recv()
        send_fx_rows(now, 1).wait_recv()
        send_rho(now).wait_recv()
        send_pot(now).wait_recv()
        send_fx_corner(now).wait_recv()
        send_pot_first(now).wait_recv()
        send_pot_rows(now, 1).wait_recv()
        send_rho_corner(now).wait_recv()
        send_rho(now).wait_send()
        send_pot(now).wait_send()
        send_fx_corner(now).wait_send()
        send_rho_corner(now).wait_send()
        send_fx_rows(now, 0).wait_send()
        send_pot_first(now).wait_send()
        lower_row = halo_row(lower, 0, now, 0, gain, jnp.where(first, jnp.zeros(TILE, jnp.float32), rho_corner[now]))
        upper_row = halo_row(upper, 0, now, 3, gain)
        scale = jnp.where(last, 1.0 / (1.0 + tau_step * end_weight), 1.0).astype(jnp.float32)
        pull = jnp.where(last, tau_step * end_weight, 0.0).astype(jnp.float32)
        above = tau_step * (pot_halo[now] - gain * upper.rho[0])
        above = jnp.concatenate([above[0:1] - (tau_step * (gain * fx_corner[now]))[None], above[1:R]], 0)
        above = jnp.where(last, jnp.zeros_like(above), above)
        before = jnp.where(first, start[...], rho_halo[now])
        lower_here = potential(lower, 0, keep, before, fx_rows[now, 0])
        lower_above = potential(lower, 1, keep, lower.rho[0], fx_rows[now, 2])
        upper_here = potential(upper, 0, keep, upper.rho[1], fx_rows[now, 1])
        update(lower, 0, 0, final, lower_here, lower_above, lower_row)
        update(upper, 0, T - 1, final, upper_here, above, upper_row, scale, pull)
        if not final:
            emit_first(later, 2.0)

    def middle_pair(u, now, later, gain, final, meet):
        keep = gain - 1.0
        if meet:
            send_pot_last(now).wait_recv()
        else:
            send_fx_rows(now, u + 1).wait_recv()
            send_pot_rows(now, u + 1).wait_recv()
        send_fx_rows(now, u).wait_send()
        send_pot_rows(now, u).wait_send()
        lower_row = halo_row(lower, u, now, 2 * u, gain)
        upper_row = halo_row(upper, u, now, 2 * u + 3, gain)
        upper_below = lower.rho[u] if meet else upper.rho[u + 1]
        upper_here = potential(upper, u, keep, upper_below, fx_rows[now, 2 * u + 1])
        lower_above = upper_here if meet else potential(lower, u + 1, keep, lower.rho[u], fx_rows[now, 2 * u + 2])
        lower_here, upper_above = lower.psi[u], upper.psi[u - 1]
        update(lower, u, u, final, lower_here, lower_above, lower_row)
        update(upper, u, T - 1 - u, final, upper_here, upper_above, upper_row)
        if not final:
            emit(later, u, 2.0)

    def iteration(now, later, gain, final):
        first_pair(now, later, gain, final)

        def pair(u, carry):
            middle_pair(u, now, later, gain, final, False)
            return carry

        lax.fori_loop(1, PAIRS - 1, pair, 0)
        middle_pair(PAIRS - 1, now, later, gain, final, True)
        send_pot_last(now).wait_send()
        if not final:
            emit_last(later, 2.0)

    def step(k, carry):
        gain = jnp.where(k == 1, 1.0, 2.0).astype(jnp.float32)
        iteration(lax.rem(k - 1, 2), lax.rem(k, 2), gain, False)
        return carry

    lax.fori_loop(1, ITERS, step, 0)
    iteration((ITERS - 1) % 2, None, 2.0, True)


def write_kernel(*refs):
    results, targets, sem = refs[:5], refs[5:10], refs[10]
    for n in range(5):
        pltpu.make_async_copy(results[n], targets[n], sem.at[n]).start()
    for n in range(5):
        pltpu.make_async_copy(results[n], targets[n], sem.at[n]).wait()


def to_rows(x):
    planes = x.shape[0]
    return x.reshape(planes, R // 8, 8, 8, 128).transpose(0, 1, 3, 2, 4).reshape(planes * R * 8, 128)


def in_hbm(x):
    return pltpu.with_memory_space_constraint(x, pltpu.HBM)


def from_rows(x):
    return x.reshape(T, R // 8, 8, 8, 128).transpose(0, 1, 3, 2, 4).reshape(T, R, 1024)


def solution(mesh):
    sizes = mesh.shape["tm"], mesh.shape["space"]
    f32 = jnp.float32
    vmem = pltpu.VMEM
    dma = pltpu.SemaphoreType.DMA

    def body(density, flux_x, flux_y, source, potential, start_density, end_density):
        anywhere = pl.BlockSpec(memory_space=pltpu.HBM)
        on_chip = pl.BlockSpec(memory_space=vmem)
        rows = T * R * 8
        results = pl.pallas_call(
            functools.partial(kernel, sizes),
            out_shape=[vmem((rows, 128), f32)] * 5,
            in_specs=[anywhere] * 7,
            out_specs=[on_chip] * 5,
            scratch_shapes=[
                vmem((5, rows, 128), f32),
                vmem((2, R * 8, 128), f32),
                [vmem((PAIRS, R) + TILE, f32)] * 7,
                [vmem((PAIRS, R) + TILE, f32)] * 7,
                vmem((R,) + TILE, f32),
                vmem((R,) + TILE, f32),
                vmem((R,) + TILE, f32),
                vmem((2 * PAIRS,) + TILE, f32),
                vmem((2 * PAIRS + 2,) + TILE, f32),
                vmem((2, R) + TILE, f32),
                vmem((2, R) + TILE, f32),
                vmem((2, 2 * PAIRS) + TILE, f32),
                vmem((2, 2 * PAIRS + 2) + TILE, f32),
                vmem((2,) + TILE, f32),
                vmem((2,) + TILE, f32),
                dma((5, T)),
                dma((2,)),
                dma((4,)),
                dma((PAIRS,)),
                dma((PAIRS + 1,)),
                dma((2, 4)),
                dma((2, PAIRS)),
                dma((2, PAIRS + 1)),
            ],
            compiler_params=pltpu.CompilerParams(
                collective_id=0, has_side_effects=True, vmem_limit_bytes=24 << 20
            ),
        )(
            *(in_hbm(to_rows(x)) for x in (density, flux_x, flux_y, source, potential)),
            in_hbm(to_rows(start_density[None])),
            in_hbm(to_rows(end_density[None])),
        )
        results = pl.pallas_call(
            write_kernel,
            out_shape=[jax.ShapeDtypeStruct((rows, 128), f32)] * 5,
            in_specs=[on_chip] * 5,
            out_specs=[anywhere] * 5,
            scratch_shapes=[dma((5,))],
            compiler_params=pltpu.CompilerParams(vmem_limit_bytes=1 << 20),
        )(*results)
        return tuple(from_rows(x) for x in results)

    volume, plane = P("tm", "space", None), P("space", None)
    return jax.shard_map(
        body, mesh=mesh, in_specs=(volume,) * 5 + (plane,) * 2, out_specs=(volume,) * 5, check_vma=False
    )
```

time: 65.5 us -> 53.3 us (0.81)
  local copies, waits for them, and re-layouts: 8.18 us -> 0 us
  Pallas kernels: 56.4 us -> 52.3 us
    unnamed x13 -> x0, local copies, waits for them, and re-layouts: 8.18 us -> none
    pallas_call x1 -> x2, Pallas kernels: 56.4 us -> 52.3 us  [the longest x1 49.9 us: body(): pl.pallas_call(functools.partial(kernel, sizes), out_shape=[vmem((rows, 1...]
where the time goes in v1:
time: 53.3 us; the launch traced here: 52.9 us
  Pallas kernels  52.3 us (98%)
  between operations  0.64 us (1%)
    pallas_call x1, Pallas kernels, body(): pl.pallas_call(functools.partial(kernel, sizes), out_shape=[vmem((rows, 1...  49.9 us
    pallas_call x1, Pallas kernels, body(): pl.pallas_call(write_kernel, out_shape=[jax.ShapeDtypeStruct((rows, 128),...  2.4 us

profile of v1, /device:TPU:1, one launch (start us, length us, event | category | flops | bytes accessed | tf_op | source)
XLA Modules:
  0.0 52.9 jit_solution(1235353530234447977)
XLA Ops:
  0.6 49.9 %shard_map.110 = (f32[2048,128]{1,0:T(8,128)S(1)}, f32[2048,128]{1,0:T(8,128)S(1)}, f32[2048,128]{1,0:T(8,128)S(1)}, f32[2048,128]{1,0:T(8,128)S(1)}, f32[2048,128]{1,0:T(8,128)S(1)}) custom-call(f32[2048,128]{1,0:T(8,128)} %bitcast.60, f32[2048,128]{1,0:T(8,128)} %bitcast.61, f32[2048,128]{1,0:T(8,128)} %bitcast.62, f32[2048,128]{1,0:T(8,128)} %bitcast.63, ...), custom_call_target="tpu_custom_call" | custom-call | tf_op jit(solution)/shard_map/pallas_call | solution.py:341
  50.5 2.4 %shard_map.111 = (f32[2048,128]{1,0:T(8,128)}, f32[2048,128]{1,0:T(8,128)}, f32[2048,128]{1,0:T(8,128)}, f32[2048,128]{1,0:T(8,128)}, f32[2048,128]{1,0:T(8,128)}) custom-call(f32[2048,128]{1,0:T(8,128)S(1)} %get-tuple-element.15.refs_0_, f32[2048,128]{1,0:T(8,128)S(1)} %get-tuple-element.16.refs_1_, f32[2048,128]{1,0:T(8,128)S(1)} %get-tuple-element.17.refs_2_, ...), custom_call_target="tpu_custom_call" | custom-call | tf_op jit(solution)/shard_map/pallas_call | solution.py:379

commit v2 on v1

--- a/solution.py
+++ b/solution.py
@@ -17,11 +17,27 @@
 T = 16
 R = 16
 PAIRS = T // 2
+TOP, BOTTOM = 4, 12
+OUTER, INNER = ((0, TOP), (BOTTOM, R)), ((TOP, BOTTOM),)
+RHO_PARTS = (0, TOP), (BOTTOM, R), (TOP, TOP + 1), (TOP + 1, BOTTOM)
+POT_PARTS = (0, TOP), (BOTTOM + 1, R), (BOTTOM, BOTTOM + 1), (TOP, BOTTOM)
 TILE = (8, 128)
 MESH = pl.DeviceIdType.MESH
 
 
 Half = collections.namedtuple("Half", ("rho", "fx", "fy", "src", "part", "pot", "psi"))
+
+
+def take(ref, u, parts):
+    values = [ref[u, a:b] for a, b in parts]
+    return values[0] if len(values) == 1 else jnp.concatenate(values, 0)
+
+
+def put(ref, u, parts, value):
+    done = 0
+    for a, b in parts:
+        ref[u, a:b] = value[done : done + b - a]
+        done += b - a
 
 
 def previous_column(x):
@@ -106,17 +122,25 @@
             device_id=device, device_id_type=MESH,
         )
 
-    def send_rho(slot):
-        return send(upper.rho.at[0], rho_halo.at[slot], plane_send.at[0], plane_recv.at[slot, 0], (time_next, me_space))
-
-    def send_pot(slot):
-        return send(plane_out, pot_halo.at[slot], plane_send.at[1], plane_recv.at[slot, 1], (time_prev, me_space))
+    def send_rho(slot, n):
+        a, b = RHO_PARTS[n]
+        rows = pl.ds(a, b - a)
+        return send(
+            upper.rho.at[0, rows], rho_halo.at[slot, rows], plane_send.at[n], plane_recv.at[slot, n], (time_next, me_space)
+        )
+
+    def send_pot(slot, n):
+        a, b = POT_PARTS[n]
+        rows = pl.ds(a, b - a)
+        return send(
+            plane_out.at[rows], pot_halo.at[slot, rows], plane_send.at[4 + n], plane_recv.at[slot, 4 + n], (time_prev, me_space)
+        )
 
     def send_fx_corner(slot):
-        return send(fx_rows_out.at[0], fx_corner.at[slot], plane_send.at[2], plane_recv.at[slot, 2], (time_prev, space_next))
+        return send(fx_rows_out.at[0], fx_corner.at[slot], plane_send.at[8], plane_recv.at[slot, 8], (time_prev, space_next))
 
     def send_rho_corner(slot):
-        return send(upper.rho.at[0, 0], rho_corner.at[slot], plane_send.at[3], plane_recv.at[slot, 3], (time_next, space_prev))
+        return send(upper.rho.at[0, 0], rho_corner.at[slot], plane_send.at[9], plane_recv.at[slot, 9], (time_next, space_prev))
 
     def send_fx_rows(slot, u):
         rows = pl.ds(2 * u, 2)
@@ -136,20 +160,30 @@
             pot_rows_out.at[rows], pot_rows.at[slot, rows], pot_send.at[PAIRS], pot_recv.at[slot, PAIRS], (me_time, space_prev)
         )
 
-    def emit_first(slot, gain):
+    def emit_outer(slot, gain):
         part, pot, fx = lower.part, lower.pot, lower.fx
-        plane_out[0] = pot[0, 0] + gain * part[0, 0]
-        plane_out[1:R] = pot[0, 1:R] + gain * (part[0, 1:R] - fx[0, 0 : R - 1])
         fx_rows_out[0] = fx[0, R - 1]
         fx_rows_out[1] = upper.fx[0, R - 1]
         held = jnp.where(first, start[0], jnp.zeros(TILE, jnp.float32))
         pot_rows_out[0] = pot[0, 0] + gain * (part[0, 0] - held)
+        plane_out[0] = pot[0, 0] + gain * part[0, 0]
+        for a, b in ((1, TOP), (BOTTOM + 1, R)):
+            plane_out[a:b] = pot[0, a:b] + gain * (part[0, a:b] - fx[0, a - 1 : b - 1])
         send_fx_corner(slot).start()
         send_rho_corner(slot).start()
         send_fx_rows(slot, 0).start()
         send_pot_first(slot).start()
-        send_pot(slot).start()
-        send_rho(slot).start()
+        for n in (0, 1):
+            send_pot(slot, n).start()
+            send_rho(slot, n).start()
+
+    def emit_inner(slot, gain):
+        part, pot, fx = lower.part, lower.pot, lower.fx
+        a, b = TOP, BOTTOM + 1
+        plane_out[a:b] = pot[0, a:b] + gain * (part[0, a:b] - fx[0, a - 1 : b - 1])
+        for n in (2, 3):
+            send_pot(slot, n).start()
+            send_rho(slot, n).start()
 
     def emit(slot, u, gain):
         fx_rows_out[2 * u] = lower.fx[u, R - 1]
@@ -187,7 +221,8 @@
     load_plane(0, lower, 0)
     load_plane(T - 1, upper, 0)
     pl.semaphore_wait(barrier, len(partners))
-    emit_first(0, 1.0)
+    emit_outer(0, 1.0)
+    emit_inner(0, 1.0)
 
     def load_pair(u, carry):
         load_plane(u, lower, u)
@@ -198,34 +233,40 @@
     lax.fori_loop(1, PAIRS, load_pair, 0)
     emit_last(0, 1.0)
 
-    def potential(half, u, keep, below, row):
-        beside = jnp.concatenate([row[None], half.fx[u, 0 : R - 1]], 0)
-        gap = half.part[u] - (below + beside)
-        base = half.pot[u] + keep * gap
-        half.pot[u] = base
+    def potential(half, u, keep, below, row, a=0, b=R):
+        if a == 0:
+            beside = jnp.concatenate([row[None], half.fx[u, 0 : b - 1]], 0)
+        else:
+            beside = half.fx[u, a - 1 : b - 1]
+        gap = half.part[u, a:b] - (below + beside)
+        base = half.pot[u, a:b] + keep * gap
+        half.pot[u, a:b] = base
         new = tau_step * (base + gap)
-        half.psi[u] = new
+        half.psi[u, a:b] = new
         return new
 
-    def update(half, u, t, final, here, above, row, end_scale=None, end_pull=None):
-        top = half.rho[u] - (here - above)
-        moved_fx = half.fx[u] - (here - jnp.concatenate([here[1:R], row[None]], 0))
-        moved_fy = half.fy[u] - (here - next_column(here))
-        moved_src = half.src[u] + here
+    def update(half, u, t, final, parts, here, above, after, end_scale=None, end_pull=None):
+        top = take(half.rho, u, parts) - (here - above)
+        moved_fx = take(half.fx, u, parts) - (here - after)
+        moved_fy = take(half.fy, u, parts) - (here - next_column(here))
+        moved_src = take(half.src, u, parts) + here
         energy = moved_fx * moved_fx + moved_fy * moved_fy + moved_src * moved_src
         if end_scale is not None:
-            top = (top - 1.0 + end_pull * end[...]) * end_scale + 1.0
+            ends = jnp.concatenate([end[a:b] for a, b in parts], 0)
+            top = (top - 1.0 + end_pull * ends) * end_scale + 1.0
             energy = energy * end_scale
         q, factor = newton(top, energy)
         new_fx, new_fy, new_src = factor * moved_fx, factor * moved_fy, factor * moved_src
         if final:
             results = tau_step * (q - 1.0), tau_step * new_fx, tau_step * new_fy, tau_step * new_src, here
+            numbers = [i for a, b in parts for i in range(a, b)]
             for ref, value in zip((rho_out, fx_out, fy_out, src_out, pot_out), results):
-                for i in range(R):
-                    ref[pl.ds(t * plane_rows + (i // 8) * 64 + i % 8, 8, stride=8), :] = value[i]
+                for n, i in enumerate(numbers):
+                    ref[pl.ds(t * plane_rows + (i // 8) * 64 + i % 8, 8, stride=8), :] = value[n]
         else:
-            half.rho[u], half.fx[u], half.fy[u], half.src[u] = q, new_fx, new_fy, new_src
-            half.part[u] = q + new_fx + (new_fy - previous_column(new_fy)) - new_src
+            new_part = q + new_fx + (new_fy - previous_column(new_fy)) - new_src
+            for ref, value in zip(half[:5], (q, new_fx, new_fy, new_src, new_part)):
+                put(ref, u, parts, value)
 
     def halo_row(half, u, slot, row, gain, corner=None):
         held = half.fx[u, R - 1]
@@ -233,37 +274,69 @@
             held = held + corner
         return tau_step * (pot_rows[slot, row] - gain * held)
 
-    def first_pair(now, later, gain, final):
+    def before(now, a, b):
+        return jnp.where(first, start[a:b], rho_halo[now, a:b])
+
+    def plane_above(now, gain, a, b):
+        value = tau_step * (pot_halo[now, a:b] - gain * upper.rho[0, a:b])
+        if a == 0:
+            corner = tau_step * (gain * fx_corner[now])
+            value = jnp.concatenate([value[0:1] - corner[None], value[1:]], 0)
+        return jnp.where(last, jnp.zeros_like(value), value)
+
+    end_scale = jnp.where(last, 1.0 / (1.0 + tau_step * end_weight), 1.0).astype(jnp.float32)
+    end_pull = jnp.where(last, tau_step * end_weight, 0.0).astype(jnp.float32)
+
+    def outer_rows(now, later, gain, final):
         keep = gain - 1.0
         send_fx_rows(now, 0).wait_recv()
         send_fx_rows(now, 1).wait_recv()
-        send_rho(now).wait_recv()
-        send_pot(now).wait_recv()
         send_fx_corner(now).wait_recv()
         send_pot_first(now).wait_recv()
         send_pot_rows(now, 1).wait_recv()
         send_rho_corner(now).wait_recv()
-        send_rho(now).wait_send()
-        send_pot(now).wait_send()
+        for n in (0, 1, 2):
+            send_rho(now, n).wait_recv()
+            send_pot(now, n).wait_recv()
+        for n in (0, 1):
+            send_rho(now, n).wait_send()
+            send_pot(now, n).wait_send()
         send_fx_corner(now).wait_send()
         send_rho_corner(now).wait_send()
         send_fx_rows(now, 0).wait_send()
         send_pot_first(now).wait_send()
         lower_row = halo_row(lower, 0, now, 0, gain, jnp.where(first, jnp.zeros(TILE, jnp.float32), rho_corner[now]))
         upper_row = halo_row(upper, 0, now, 3, gain)
-        scale = jnp.where(last, 1.0 / (1.0 + tau_step * end_weight), 1.0).astype(jnp.float32)
-        pull = jnp.where(last, tau_step * end_weight, 0.0).astype(jnp.float32)
-        above = tau_step * (pot_halo[now] - gain * upper.rho[0])
-        above = jnp.concatenate([above[0:1] - (tau_step * (gain * fx_corner[now]))[None], above[1:R]], 0)
-        above = jnp.where(last, jnp.zeros_like(above), above)
-        before = jnp.where(first, start[...], rho_halo[now])
-        lower_here = potential(lower, 0, keep, before, fx_rows[now, 0])
         lower_above = potential(lower, 1, keep, lower.rho[0], fx_rows[now, 2])
         upper_here = potential(upper, 0, keep, upper.rho[1], fx_rows[now, 1])
-        update(lower, 0, 0, final, lower_here, lower_above, lower_row)
-        update(upper, 0, T - 1, final, upper_here, above, upper_row, scale, pull)
+        over = potential(lower, 0, keep, before(now, 0, TOP + 1), fx_rows[now, 0], 0, TOP + 1)
+        under = potential(lower, 0, keep, before(now, BOTTOM, R), None, BOTTOM, R)
+        here = jnp.concatenate([over[0:TOP], under], 0)
+        after = jnp.concatenate([over[1 : TOP + 1], under[1:], lower_row[None]], 0)
+        above = jnp.concatenate([lower_above[0:TOP], lower_above[BOTTOM:R]], 0)
+        update(lower, 0, 0, final, OUTER, here, above, after)
+        here = jnp.concatenate([upper_here[0:TOP], upper_here[BOTTOM:R]], 0)
+        after = jnp.concatenate([upper_here[1 : TOP + 1], upper_here[BOTTOM + 1 : R], upper_row[None]], 0)
+        above = jnp.concatenate([plane_above(now, gain, 0, TOP), plane_above(now, gain, BOTTOM, R)], 0)
+        update(upper, 0, T - 1, final, OUTER, here, above, after, end_scale, end_pull)
         if not final:
-            emit_first(later, 2.0)
+            emit_outer(later, 2.0)
+
+    def inner_rows(now, later, gain, final):
+        send_rho(now, 3).wait_recv()
+        send_pot(now, 3).wait_recv()
+        for n in (2, 3):
+            send_rho(now, n).wait_send()
+            send_pot(now, n).wait_send()
+        a, b = TOP, BOTTOM
+        rest = potential(lower, 0, gain - 1.0, before(now, a + 1, b), None, a + 1, b)
+        here = jnp.concatenate([lower.psi[0, a : a + 1], rest], 0)
+        after = jnp.concatenate([rest, lower.psi[0, b : b + 1]], 0)
+        update(lower, 0, 0, final, INNER, here, lower.psi[1, a:b], after)
+        here, after = upper.psi[0, a:b], upper.psi[0, a + 1 : b + 1]
+        update(upper, 0, T - 1, final, INNER, here, plane_above(now, gain, a, b), after, end_scale, end_pull)
+        if not final:
+            emit_inner(later, 2.0)
 
     def middle_pair(u, now, later, gain, final, meet):
         keep = gain - 1.0
@@ -280,15 +353,22 @@
         upper_here = potential(upper, u, keep, upper_below, fx_rows[now, 2 * u + 1])
         lower_above = upper_here if meet else potential(lower, u + 1, keep, lower.rho[u], fx_rows[now, 2 * u + 2])
         lower_here, upper_above = lower.psi[u], upper.psi[u - 1]
-        update(lower, u, u, final, lower_here, lower_above, lower_row)
-        update(upper, u, T - 1 - u, final, upper_here, upper_above, upper_row)
+        whole = ((0, R),)
+        after = jnp.concatenate([lower_here[1:R], lower_row[None]], 0)
+        update(lower, u, u, final, whole, lower_here, lower_above, after)
+        after = jnp.concatenate([upper_here[1:R], upper_row[None]], 0)
+        update(upper, u, T - 1 - u, final, whole, upper_here, upper_above, after)
         if not final:
             emit(later, u, 2.0)
 
     def iteration(now, later, gain, final):
-        first_pair(now, later, gain, final)
+        outer_rows(now, later, gain, final)
 
         def pair(u, carry):
+            @pl.when(u == 2)
+            def _():
+                inner_rows(now, later, gain, final)
+
             middle_pair(u, now, later, gain, final, False)
             return carry
 
@@ -361,10 +441,10 @@
                 vmem((2,) + TILE, f32),
                 dma((5, T)),
                 dma((2,)),
-                dma((4,)),
+                dma((10,)),
                 dma((PAIRS,)),
                 dma((PAIRS + 1,)),
-                dma((2, 4)),
+                dma((2, 10)),
                 dma((2, PAIRS)),
                 dma((2, PAIRS + 1)),
             ],

time: 53.3 us -> 49.7 us (0.932)
  Pallas kernels: 52.3 us -> 48.9 us
    pallas_call x1, Pallas kernels: 49.9 us -> 46.5 us  [body(): pl.pallas_call(functools.partial(kernel, sizes), out_shape=[vmem((rows, 1...]
where the time goes in v2:
time: 49.7 us; the launch traced here: 49.6 us
  Pallas kernels  48.9 us (98%)
  between operations  0.64 us (1%)
    pallas_call x1, Pallas kernels, body(): pl.pallas_call(functools.partial(kernel, sizes), out_shape=[vmem((rows, 1...  46.5 us
    pallas_call x1, Pallas kernels, body(): pl.pallas_call(write_kernel, out_shape=[jax.ShapeDtypeStruct((rows, 128),...  2.4 us

profile of v2, /device:TPU:1, one launch (start us, length us, event | category | flops | bytes accessed | tf_op | source)
XLA Modules:
  0.0 49.6 jit_solution(10344083128842169221)
XLA Ops:
  0.6 46.5 %shard_map.110 = (f32[2048,128]{1,0:T(8,128)S(1)}, f32[2048,128]{1,0:T(8,128)S(1)}, f32[2048,128]{1,0:T(8,128)S(1)}, f32[2048,128]{1,0:T(8,128)S(1)}, f32[2048,128]{1,0:T(8,128)S(1)}) custom-call(f32[2048,128]{1,0:T(8,128)} %bitcast.60, f32[2048,128]{1,0:T(8,128)} %bitcast.61, f32[2048,128]{1,0:T(8,128)} %bitcast.62, f32[2048,128]{1,0:T(8,128)} %bitcast.63, ...), custom_call_target="tpu_custom_call" | custom-call | tf_op jit(solution)/shard_map/pallas_call | solution.py:421
  47.2 2.4 %shard_map.111 = (f32[2048,128]{1,0:T(8,128)}, f32[2048,128]{1,0:T(8,128)}, f32[2048,128]{1,0:T(8,128)}, f32[2048,128]{1,0:T(8,128)}, f32[2048,128]{1,0:T(8,128)}) custom-call(f32[2048,128]{1,0:T(8,128)S(1)} %get-tuple-element.15.refs_0_, f32[2048,128]{1,0:T(8,128)S(1)} %get-tuple-element.16.refs_1_, f32[2048,128]{1,0:T(8,128)S(1)} %get-tuple-element.17.refs_2_, ...), custom_call_target="tpu_custom_call" | custom-call | tf_op jit(solution)/shard_map/pallas_call | solution.py:459

commit v3 on v2

--- a/solution.py
+++ b/solution.py
@@ -322,12 +322,14 @@
         if not final:
             emit_outer(later, 2.0)
 
-    def inner_rows(now, later, gain, final):
+    def inner_waits(now):
         send_rho(now, 3).wait_recv()
         send_pot(now, 3).wait_recv()
         for n in (2, 3):
             send_rho(now, n).wait_send()
             send_pot(now, n).wait_send()
+
+    def inner_rows(now, gain, final):
         a, b = TOP, BOTTOM
         rest = potential(lower, 0, gain - 1.0, before(now, a + 1, b), None, a + 1, b)
         here = jnp.concatenate([lower.psi[0, a : a + 1], rest], 0)
@@ -335,11 +337,11 @@
         update(lower, 0, 0, final, INNER, here, lower.psi[1, a:b], after)
         here, after = upper.psi[0, a:b], upper.psi[0, a + 1 : b + 1]
         update(upper, 0, T - 1, final, INNER, here, plane_above(now, gain, a, b), after, end_scale, end_pull)
-        if not final:
-            emit_inner(later, 2.0)
-
-    def middle_pair(u, now, later, gain, final, meet):
+
+    def middle_pair(u, now, later, gain, final, meet, inner=False):
         keep = gain - 1.0
+        if inner:
+            inner_waits(now)
         if meet:
             send_pot_last(now).wait_recv()
         else:
@@ -353,6 +355,8 @@
         upper_here = potential(upper, u, keep, upper_below, fx_rows[now, 2 * u + 1])
         lower_above = upper_here if meet else potential(lower, u + 1, keep, lower.rho[u], fx_rows[now, 2 * u + 2])
         lower_here, upper_above = lower.psi[u], upper.psi[u - 1]
+        if inner:
+            inner_rows(now, gain, final)
         whole = ((0, R),)
         after = jnp.concatenate([lower_here[1:R], lower_row[None]], 0)
         update(lower, u, u, final, whole, lower_here, lower_above, after)
@@ -360,19 +364,19 @@
         update(upper, u, T - 1 - u, final, whole, upper_here, upper_above, after)
         if not final:
             emit(later, u, 2.0)
+            if inner:
+                emit_inner(later, 2.0)
 
     def iteration(now, later, gain, final):
         outer_rows(now, later, gain, final)
 
         def pair(u, carry):
-            @pl.when(u == 2)
-            def _():
-                inner_rows(now, later, gain, final)
-
             middle_pair(u, now, later, gain, final, False)
             return carry
 
-        lax.fori_loop(1, PAIRS - 1, pair, 0)
+        middle_pair(1, now, later, gain, final, False)
+        middle_pair(2, now, later, gain, final, False, True)
+        lax.fori_loop(3, PAIRS - 1, pair, 0)
         middle_pair(PAIRS - 1, now, later, gain, final, True)
         send_pot_last(now).wait_send()
         if not final:

time: 49.7 us -> 50 us (level)
  no operation moved by 1% of the time
where the time goes in v3:
time: 50 us; the launch traced here: 49.9 us
  Pallas kernels  49.3 us (99%)
  between operations  0.64 us (1%)
    pallas_call x1, Pallas kernels, body(): pl.pallas_call(functools.partial(kernel, sizes), out_shape=[vmem((rows, 1...  46.9 us
    pallas_call x1, Pallas kernels, body(): pl.pallas_call(write_kernel, out_shape=[jax.ShapeDtypeStruct((rows, 128),...  2.4 us

profile of v3, /device:TPU:1, one launch (start us, length us, event | category | flops | bytes accessed | tf_op | source)
XLA Modules:
  0.0 49.9 jit_solution(16233076562803093606)
XLA Ops:
  0.6 46.9 %shard_map.110 = (f32[2048,128]{1,0:T(8,128)S(1)}, f32[2048,128]{1,0:T(8,128)S(1)}, f32[2048,128]{1,0:T(8,128)S(1)}, f32[2048,128]{1,0:T(8,128)S(1)}, f32[2048,128]{1,0:T(8,128)S(1)}) custom-call(f32[2048,128]{1,0:T(8,128)} %bitcast.60, f32[2048,128]{1,0:T(8,128)} %bitcast.61, f32[2048,128]{1,0:T(8,128)} %bitcast.62, f32[2048,128]{1,0:T(8,128)} %bitcast.63, ...), custom_call_target="tpu_custom_call" | custom-call | tf_op jit(solution)/shard_map/pallas_call | solution.py:425
  47.5 2.4 %shard_map.111 = (f32[2048,128]{1,0:T(8,128)}, f32[2048,128]{1,0:T(8,128)}, f32[2048,128]{1,0:T(8,128)}, f32[2048,128]{1,0:T(8,128)}, f32[2048,128]{1,0:T(8,128)}) custom-call(f32[2048,128]{1,0:T(8,128)S(1)} %get-tuple-element.15.refs_0_, f32[2048,128]{1,0:T(8,128)S(1)} %get-tuple-element.16.refs_1_, f32[2048,128]{1,0:T(8,128)S(1)} %get-tuple-element.17.refs_2_, ...), custom_call_target="tpu_custom_call" | custom-call | tf_op jit(solution)/shard_map/pallas_call | solution.py:463
